TPU v7x, 256 devices: a whole 4x4x8 slice. The times are simulated.
256 devices in a mesh: tile: 4 (over z_lo, core), freq: 64 (over y, z_hi, x).
Axes of the slice: x: 4, y: 4, z: 8 (z_hi: 4, z_lo: 2; z = z_hi * 2 + z_lo), core: 2. Of those that a mesh axis runs over, the one named last changes fastest.
Arguments:
- sky: bfloat16 [4, 512, 2, 4096], P('tile', 'freq'), may hold values from -6 to 6
- kernel: bfloat16 [4, 64, 2, 4096, 128], P('tile', 'freq'), may hold values from -0.0625 to 0.0625
- data: bfloat16 [64, 2, 128, 512], P('freq'), may hold values from -6 to 6
- block_tiles: int32 [64, 4], P('freq'), may hold values 0 or 1
- length_bin: int32 [64, 128], P('freq'), may hold values from 0 to 31
- wedge_keep: int32 [32, 512], replicated, may hold values 0 or 1
Outputs:
- gradient: float32 [4, 512, 2, 4096], P('tile', 'freq')
All inputs are finite; a program needn't handle non-finite values. No bound on the sum of `block_tiles` on one device may be relied on, other than what follows from the above.
Results may differ from a plain program's by a relative error of at most 0.0027.
Values may be sent and summed in bfloat16 or wider, within the bound.
A program may use at most 128 MiB of HBM per device.

v0:
```python
import math
import jax
import jax.numpy as jnp
from jax import lax
from jax.sharding import Mesh
from jax.sharding import PartitionSpec as P

FREQ = ("freq_0", "freq_1", "freq_2")


def sent_to_all(shard, axis):
    copies = jnp.broadcast_to(shard, (lax.axis_size(axis), *shard.shape))
    return lax.all_to_all(copies, axis, split_axis=0, concat_axis=0, tiled=True)


def of_everyone(shard, axis):
    return sent_to_all(shard, axis).sum(axis=0)


def own_block(tiles, axes, sequence):
    dims = [lax.axis_size(a) for a in axes]
    tiles = tiles.reshape(*dims, *tiles.shape[1:])
    tiles = tiles.transpose(*sequence, *range(len(axes), tiles.ndim))
    tiles = tiles.reshape(-1, *tiles.shape[len(axes) :])
    for k in sequence:
        tiles = lax.psum_scatter(tiles, axes[k], scatter_dimension=0, tiled=True)
    return tiles[0]


def in_blocks(shard, dim, count):
    before, after = (shard.shape[:dim], shard.shape[dim + 1 :])
    return jnp.moveaxis(shard.reshape(*before, count, -1, *after), dim, 0)


def scatter_axes(shard, axes, sequence, dim):
    count = lax.axis_size(axes)
    return own_block(in_blocks(shard, dim, count), axes, sequence)


def delay_tables(length):
    indices = jnp.arange(length, dtype=jnp.int32)
    product = indices[:, None] * indices[None, :] % length
    angle = product.astype(jnp.float32) * (2.0 * math.pi / length)
    return (jnp.cos(angle), jnp.sin(angle))


def real_form(kernel_pair):
    upper_half = jnp.concatenate([kernel_pair[0], kernel_pair[1]], axis=1)
    lower_half = jnp.concatenate([-kernel_pair[1], kernel_pair[0]], axis=1)
    return jnp.concatenate([upper_half, lower_half], axis=0)


def transform(values, table):
    return jnp.einsum("...c,ck->...k", values, table, precision=lax.Precision.HIGHEST)


def keep_table(own_bins, wedge_keep):
    levels = jnp.arange(wedge_keep.shape[0], dtype=jnp.int32)
    one_hot = (own_bins[:, :, None] == levels[None, None, :]).astype(jnp.float32)
    return jnp.einsum(
        "jbl,lk->jbk", one_hot, wedge_keep.astype(jnp.float32), precision=lax.Precision.HIGHEST
    )


def back_project(visibility, data, keep_mask, cosine, sine_table):
    norm_factor = 1.0 / math.sqrt(cosine.shape[0])
    real_vis = visibility[:, 0]
    imag_vis = visibility[:, 1]
    spec_real = (transform(real_vis, cosine) + transform(imag_vis, sine_table)) * norm_factor
    spec_imag = (transform(imag_vis, cosine) - transform(real_vis, sine_table)) * norm_factor
    miss_real = keep_mask * (spec_real - data[:, 0].astype(jnp.float32))
    miss_imag = keep_mask * (spec_imag - data[:, 1].astype(jnp.float32))
    back_real = (transform(miss_real, cosine) - transform(miss_imag, sine_table)) * norm_factor
    back_imag = (transform(miss_imag, cosine) + transform(miss_real, sine_table)) * norm_factor
    return jnp.stack([back_real, back_imag], axis=1).astype(jnp.bfloat16)


def body(sky, kernel, data, block_tiles, length_bin, wedge_keep):
    channels = data.shape[3]
    blocks = kernel.shape[1]
    cell_count = kernel.shape[3]
    base_count = kernel.shape[4]
    local_channels = sky.shape[1]
    tile_pos = lax.axis_index("tile")
    column = jnp.arange(block_tiles.shape[1], dtype=jnp.int32) == tile_pos
    weights = jnp.sum(jnp.where(column[None, :], block_tiles, 0), axis=1).astype(jnp.float32)
    real_forms = jax.vmap(real_form)(kernel[0])
    sky_piece = lax.all_gather(sky, FREQ, axis=1, tiled=True)
    flat_rows = sky_piece[0].reshape(sky_piece.shape[1], 2 * cell_count)
    visibility = jnp.einsum(
        "nc,jcb->jbn", flat_rows, real_forms, preferred_element_type=jnp.float32
    )
    partial_vis = visibility * weights[:, None, None]
    cosine, sine_table = delay_tables(channels)
    visibility = of_everyone(partial_vis, "tile").reshape(blocks, 2, base_count, channels)
    back_field = back_project(
        visibility, data, keep_table(length_bin, wedge_keep), cosine, sine_table
    )
    scaled = (back_field * weights[:, None, None, None].astype(jnp.bfloat16)).reshape(
        blocks, 2 * base_count, channels
    )
    partial_value = jnp.einsum(
        "jpn,jcp->nc", scaled, real_forms, preferred_element_type=jnp.float32
    )
    gradient = scatter_axes(
        partial_value.reshape(local_channels * lax.axis_size(FREQ), 2, cell_count),
        FREQ,
        (0, 2, 1),
        0,
    )
    return gradient[None]


def solution(mesh):
    finer = Mesh(
        mesh.devices.reshape(mesh.shape["tile"], 4, 4, 4), ("tile", "freq_0", "freq_1", "freq_2")
    )
    return jax.shard_map(
        body,
        mesh=finer,
        in_specs=(
            P("tile", FREQ, None, None),
            P("tile", FREQ, None, None, None),
            P(FREQ, None, None, None),
            P(FREQ, None),
            P(FREQ, None),
            P(),
        ),
        out_specs=P("tile", FREQ, None, None),
        check_vma=False,
    )
```

profile of v0, /device:TPU:8, one launch (start us, length us, event | category | flops | bytes accessed | tf_op | source)
XLA Modules:
  0.0 477.6 jit_solution(9158189896188263960)
XLA Ops:
  6.5 0.0 all-gather.2.cloned.1.call-start
  6.5 0.7 all-gather.2.cloned.1.call-update
  7.3 1.3 fusion.40
  9.2 1.4 fusion.73
  10.6 1.7 slice_bitcast_fusion
  12.3 0.0 copy-start
  12.3 0.0 copy-start.1
  12.3 108.5 %all-gather.2.cloned.1.call-done = bf16[1,512,2,4096]{3,2,0,1:T(2,128)(2,1)} async-done(((bf16[1,8,2,4096]{3,2,0,1:T(2,128)(2,1)}), bf16[1,512,2,4096]{3,2,0,1:T(2,128)(2,1)}) %all-gather.2.cloned.1.call-update) | async-done | bytes 8388624 | tf_op jit(solution)/shard_map/all_gather | solution.py:88
  120.7 16.2 %copy.21 = bf16[64,8,2,4096]{3,1,2,0:T(8,128)(2,1)} copy(bf16[64,8,2,4096]{3,2,1,0:T(2,128)(2,1)} %bitcast.61) | data formatting | bytes 16777216
  136.9 0.0 copy-done
  136.9 0.0 copy-done.1
  137.0 0.0 copy-start.2
  137.0 0.0 copy-start.3
  137.0 6.3 %fusion.2 = f32[256,512]{1,0:T(8,128)S(1)} fusion(bf16[512,8192]{1,0:T(8,128)(2,1)} %bitcast.62, f32[]{:T(128)S(6)} %convert_element_type.51, bf16[1,4096,128]{2,1,0:T(8,128)(2,1)S(1)} %get-tuple-element.6, bf16[1,4096,128]{2,1,0:T(8,128)(2,1)S(1)} %fusion.73, bf16[1,4096,128]{2,1,0:T(8,128)(2,1)S(1)} %get-tuple-element.5), kind=kOutput, calls=%fused_computation.7 | convolution fusion | flops 2164391936 | bytes 12058628 | tf_op jit(solution)/shard_map/nc,jcb->jbn/dot_general | solution.py:90
  143.3 1.6 broadcast_in_dim.7
  144.9 10.2 %all-to-all-start = ((f32[4,1,256,512]{3,2,1,0:T(8,128)}), f32[4,1,256,512]{3,2,1,0:T(8,128)S(1)}, u32[]{:S(2)}, u32[]{:S(2)}) async-start(f32[4,1,256,512]{3,2,1,0:T(8,128)} %broadcast_in_dim.7), calls=%async_computation | async-start | bytes 4194304 | tf_op jit(solution)/shard_map/all_to_all | solution.py:13
  155.1 0.0 reduce-scatter.4.cloned.1.call-start
  155.1 0.0 copy-done.2
  155.1 0.0 copy-done.3
  155.1 0.3 fusion.37
  155.4 10.9 %maximum_maximum_fusion = bf16[1,8192,256]{2,1,0:T(8,128)(2,1)} fusion(bf16[1,4096,128]{2,1,0:T(8,128)(2,1)} %copy-done.1, bf16[1,4096,128]{2,1,0:T(8,128)(2,1)S(1)} %fusion.73, bf16[1,4096,128]{2,1,0:T(8,128)(2,1)} %copy-done), kind=kLoop, calls=%fused_computation.1 | loop fusion | flops 16777216 | bytes 7340032 | tf_op jit(solution)/shard_map/vmap()/concatenate | solution.py:50
  166.2 0.0 copy-start.4
  166.2 14.7 %all-to-all-done = f32[4,1,256,512]{3,2,1,0:T(8,128)S(1)} async-done(((f32[4,1,256,512]{3,2,1,0:T(8,128)}), f32[4,1,256,512]{3,2,1,0:T(8,128)S(1)}, u32[]{:S(2)}, u32[]{:S(2)}) %all-to-all-start) | async-done | bytes 2097184 | tf_op jit(solution)/shard_map/all_to_all | solution.py:13
  180.9 0.2 reduce_sum.19
  181.1 4.9 %fusion.27 = f32[128,512]{1,0:T(8,128)S(1)} fusion(f32[1,2,128,512]{3,2,1,0:T(8,128)S(1)} %bitcast.67), kind=kOutput, calls=%fused_computation.35 | convolution fusion | flops 406323200 | bytes 524288 | tf_op jit(solution)/shard_map/...c,ck->...k/dot_general | solution.py:54
  186.0 4.9 %fusion.31 = f32[128,512]{1,0:T(8,128)S(1)} fusion(f32[1,2,128,512]{3,2,1,0:T(8,128)S(1)} %bitcast.68), kind=kOutput, calls=%fused_computation.37 | convolution fusion | flops 406323200 | bytes 524288 | tf_op jit(solution)/shard_map/...c,ck->...k/dot_general | solution.py:54
  190.9 0.0 copy-done.4
  190.9 4.9 %fusion.9 = f32[128,512]{1,0:T(8,128)S(1)} fusion(f32[128,512]{1,0:T(8,128)S(1)} %fusion.37, f32[128,512]{1,0:T(8,128)S(1)} %fusion.27, f32[1,2,128,512]{3,2,1,0:T(8,128)S(1)} %bitcast.69, bf16[1,2,128,512]{3,2,1,0:T(8,128)(2,1)S(1)} %copy-done.4), kind=kOutput, calls=%fused_computation.15 | convolution fusion | flops 406650880 | bytes 1179648 | tf_op jit(solution)/shard_map/...c,ck->...k/dot_general | solution.py:54
  195.7 5.0 %fusion.25 = f32[128,512]{1,0:T(8,128)S(1)} fusion(f32[128,512]{1,0:T(8,128)S(1)} %fusion.9), kind=kOutput, calls=%fused_computation.34 | convolution fusion | flops 406323200 | bytes 524288 | tf_op jit(solution)/shard_map/...c,ck->...k/dot_general | solution.py:54
  200.8 4.9 %fusion.12 = f32[128,512]{1,0:T(8,128)S(1)} fusion(f32[128,512]{1,0:T(8,128)S(1)} %fusion.37, f32[128,512]{1,0:T(8,128)S(1)} %fusion.31, f32[1,2,128,512]{3,2,1,0:T(8,128)S(1)} %bitcast.70, bf16[1,2,128,512]{3,2,1,0:T(8,128)(2,1)S(1)} %copy-done.4), kind=kOutput, calls=%fused_computation.19 | convolution fusion | flops 406650880 | bytes 1179648 | tf_op jit(solution)/shard_map/...c,ck->...k/dot_general | solution.py:54
  205.7 4.9 %fusion.29 = f32[128,512]{1,0:T(8,128)S(1)} fusion(f32[128,512]{1,0:T(8,128)S(1)} %fusion.12), kind=kOutput, calls=%fused_computation.36 | convolution fusion | flops 406323200 | bytes 524288 | tf_op jit(solution)/shard_map/...c,ck->...k/dot_general | solution.py:54
  210.5 4.7 fusion.15
  215.3 4.9 %fusion.16 = bf16[1,1,128,512]{3,2,1,0:T(8,128)(2,1)S(1)} fusion(f32[128,512]{1,0:T(8,128)S(1)} %fusion.29, f32[128,512]{1,0:T(8,128)S(1)} %fusion.9), kind=kOutput, calls=%fused_computation.23 | convolution fusion | flops 406519808 | bytes 655360 | tf_op jit(solution)/shard_map/...c,ck->...k/dot_general | solution.py:54
  220.3 0.1 copy.16
  220.4 4.6 convolution_bitcast_fusion
  225.0 6.2 %copy.17 = f32[4,4,4,8,2,4096]{5,3,4,2,1,0:T(8,128)} copy(f32[4,4,4,8,2,4096]{5,3,4,1,2,0:T(8,128)S(1)} %convolution_bitcast_fusion) | data formatting | bytes 33554432 | tf_op jit(solution)/shard_map/transpose | solution.py:23
  231.2 0.0 reduce-scatter.4.cloned.1.call-update
  231.2 0.0 reduce-scatter.6.cloned.1.call-start
  231.2 148.6 %reduce-scatter.4.cloned.1.call-done = f32[16,8,2,4096]{3,1,2,0:T(8,128)} async-done(((f32[64,8,2,4096]{3,1,2,0:T(8,128)}), f32[16,8,2,4096]{3,1,2,0:T(8,128)}) %reduce-scatter.4.cloned.1.call-update) | async-done | bytes 4194320 | tf_op jit(solution)/shard_map/reduce_scatter | solution.py:26
  379.8 0.0 reduce-scatter.6.cloned.1.call-update
  379.9 0.0 reduce-scatter.8.cloned.1.call-start
  379.9 52.9 %reduce-scatter.6.cloned.1.call-done = f32[4,8,2,4096]{3,1,2,0:T(8,128)} async-done(((f32[16,8,2,4096]{3,1,2,0:T(8,128)}), f32[4,8,2,4096]{3,1,2,0:T(8,128)}) %reduce-scatter.6.cloned.1.call-update) | async-done | bytes 1048592 | tf_op jit(solution)/shard_map/reduce_scatter | solution.py:26
  432.8 0.0 reduce-scatter.8.cloned.1.call-update
  432.8 36.3 %reduce-scatter.8.cloned.1.call-done = f32[1,8,2,4096]{3,1,2,0:T(8,128)} async-done(((f32[4,8,2,4096]{3,1,2,0:T(8,128)}), f32[1,8,2,4096]{3,1,2,0:T(8,128)}) %reduce-scatter.8.cloned.1.call-update) | async-done | bytes 262160 | tf_op jit(solution)/shard_map/reduce_scatter | solution.py:26
  469.0 1.9 copy.18
  (1 shorter events, 0.0 us)
Async XLA Ops:
  6.5 114.2 %all-gather.2.cloned.1.call-start = ((), (), s32[]{:S(2)}) async-start(), calls=%async_computation.4 | async-start | bytes 8519680 | tf_op jit(solution)/shard_map/all_gather | solution.py:88
  12.3 124.7 %copy-start = (bf16[1,4096,128]{2,1,0:T(8,128)(2,1)}, bf16[1,4096,128]{2,1,0:T(8,128)(2,1)S(1)}, u32[]{:S(2)}) copy-start(bf16[1,4096,128]{2,1,0:T(8,128)(2,1)S(1)} %get-tuple-element.5) | copy-start | bytes 3145732
  12.3 124.7 %copy-start.1 = (bf16[1,4096,128]{2,1,0:T(8,128)(2,1)}, bf16[1,4096,128]{2,1,0:T(8,128)(2,1)S(1)}, u32[]{:S(2)}) copy-start(bf16[1,4096,128]{2,1,0:T(8,128)(2,1)S(1)} %get-tuple-element.6) | copy-start | bytes 3145732
  137.0 18.1 %copy-start.2 = (s32[32,512]{1,0:T(8,128)S(1)}, s32[32,512]{1,0:T(8,128)}, u32[]{:S(2)}) copy-start(s32[32,512]{1,0:T(8,128)} %param.11) | copy-start | bytes 196612
  137.0 18.1 %copy-start.3 = (s32[1,128]{1,0:T(1,128)S(1)}, s32[1,128]{1,0:T(1,128)}, u32[]{:S(2)}) copy-start(s32[1,128]{1,0:T(1,128)} %param.10) | copy-start | bytes 1540
  144.9 36.0 %all-to-all-start = ((f32[4,1,256,512]{3,2,1,0:T(8,128)}), f32[4,1,256,512]{3,2,1,0:T(8,128)S(1)}, u32[]{:S(2)}, u32[]{:S(2)}) async-start(f32[4,1,256,512]{3,2,1,0:T(8,128)} %broadcast_in_dim.7), calls=%async_computation | async-start | bytes 4194304 | tf_op jit(solution)/shard_map/all_to_all | solution.py:13
  155.1 224.8 %reduce-scatter.4.cloned.1.call-start = ((), (), s32[]{:S(2)}) async-start(), calls=%async_computation.5 | async-start | bytes 20971520 | tf_op jit(solution)/shard_map/reduce_scatter | solution.py:26
  166.2 24.6 %copy-start.4 = (bf16[1,2,128,512]{3,2,1,0:T(8,128)(2,1)S(1)}, bf16[1,2,128,512]{3,2,1,0:T(8,128)(2,1)}, u32[]{:S(2)}) copy-start(bf16[1,2,128,512]{3,2,1,0:T(8,128)(2,1)} %param.8) | copy-start | bytes 786436
  231.2 201.6 %reduce-scatter.6.cloned.1.call-start = ((), (), s32[]{:S(2)}) async-start(), calls=%async_computation.6 | async-start | bytes 5242880 | tf_op jit(solution)/shard_map/reduce_scatter | solution.py:26
  379.9 89.2 %reduce-scatter.8.cloned.1.call-start = ((), (), s32[]{:S(2)}) async-start(), calls=%async_computation.7 | async-start | bytes 1310720 | tf_op jit(solution)/shard_map/reduce_scatter | solution.py:26
Sparse Core Ops, SparseCore 0:
  10.6 110.0 all-gather.1
  231.3 148.4 reduce-scatter.3
  382.4 50.3 reduce-scatter.5
  435.2 33.8 reduce-scatter.7
where the time goes:
time: 487 us; the launch traced here: 478 us
  waiting for transfers between devices  362 us (74%)
  matrix products  50.2 us (10%)
  local copies, waits for them, and re-layouts  27.7 us (6%)
  between operations  14.2 us (3%)
  other arithmetic  13.8 us (3%)
  starting transfers between devices  10.3 us (2%)
    reduce_scatter x3, waiting for transfers between devices, own_block(): tiles = lax.psum_scatter(tiles, axes[k], scatter_dimension=0, tiled=True)  238 us
    all_gather x1, waiting for transfers between devices, body(): sky_piece = lax.all_gather(sky, FREQ, axis=1, tiled=True)  108 us
    dot_general x8, matrix products, transform(): jnp.einsum('...c,ck->...k', values, table, precision=lax.Precision.HIGHEST)  39 us
    unnamed x11, local copies, waits for them, and re-layouts  16.2 us
    all_to_all x1, waiting for transfers between devices, sent_to_all(): return lax.all_to_all(copies, axis, split_axis=0, concat_axis=0, tiled=True)  14.7 us
    concatenate x1, other arithmetic, real_form(): return jnp.concatenate([upper_half, lower_half], axis=0)  10.9 us
    all_to_all x1, starting transfers between devices, sent_to_all(): return lax.all_to_all(copies, axis, split_axis=0, concat_axis=0, tiled=True)  10.2 us
  transfers between devices with their start and end apart: 5, of which 5 were waited for; matrix products, arithmetic and copies ran while one was open for 3% of the time, Pallas kernels for 0%

commit v1 on v0

--- a/solution.py
+++ b/solution.py
@@ -85,7 +85,8 @@
     column = jnp.arange(block_tiles.shape[1], dtype=jnp.int32) == tile_pos
     weights = jnp.sum(jnp.where(column[None, :], block_tiles, 0), axis=1).astype(jnp.float32)
     real_forms = jax.vmap(real_form)(kernel[0])
-    sky_piece = lax.all_gather(sky, FREQ, axis=1, tiled=True)
+    stack = jnp.stack([sky] * lax.axis_size(FREQ))
+    sky_piece = jnp.concatenate(lax.all_to_all(stack, FREQ, 0, 0), axis=1)
     flat_rows = sky_piece[0].reshape(sky_piece.shape[1], 2 * cell_count)
     visibility = jnp.einsum(
         "nc,jcb->jbn", flat_rows, real_forms, preferred_element_type=jnp.float32

time: 487 us -> 574 us (1.18)
  waiting for transfers between devices: 362 us -> 435 us
  starting transfers between devices: 10.3 us -> 19 us
  local copies, waits for them, and re-layouts: 27.7 us -> 34.1 us
    all_to_all x0 -> x1, waiting for transfers between devices: none -> 182 us  [body(): sky_piece = jnp.concatenate(lax.all_to_all(stack, FREQ, 0, 0), axis=1)]
    all_gather x1 -> x0, waiting for transfers between devices: 108 us -> none  [body(): sky_piece = lax.all_gather(sky, FREQ, axis=1, tiled=True)]
    all_to_all x0 -> x1, starting transfers between devices: none -> 14.9 us  [body(): sky_piece = jnp.concatenate(lax.all_to_all(stack, FREQ, 0, 0), axis=1)]
    another operation x0 -> x1, local copies, waits for them, and re-layouts: none -> 6.42 us  [body(): stack = jnp.stack([sky] * lax.axis_size(FREQ))]
    all_to_all x1, starting transfers between devices: 10.2 us -> 4.01 us  [sent_to_all(): return lax.all_to_all(copies, axis, split_axis=0, concat_axis=0, tiled=True)]
    unnamed x11 -> x15, local copies, waits for them, and re-layouts: 16.2 us -> 16.4 us
  transfers between devices with their start and end apart: 5 -> 5, of which waited for: 5 -> 5; matrix products, arithmetic and copies ran while one was open for 3% -> 2% of each run, Pallas kernels for 0% -> 0%
where the time goes in v1:
time: 574 us; the launch traced here: 564 us
  waiting for transfers between devices  435 us (76%)
  matrix products  50 us (9%)
  local copies, waits for them, and re-layouts  34.1 us (6%)
  starting transfers between devices  19 us (3%)
  between operations  14.4 us (3%)
  other arithmetic  11.9 us (2%)
    reduce_scatter x3, waiting for transfers between devices, own_block(): tiles = lax.psum_scatter(tiles, axes[k], scatter_dimension=0, tiled=True)  239 us
    all_to_all x1, waiting for transfers between devices, body(): sky_piece = jnp.concatenate(lax.all_to_all(stack, FREQ, 0, 0), axis=1)  182 us
    dot_general x8, matrix products, transform(): jnp.einsum('...c,ck->...k', values, table, precision=lax.Precision.HIGHEST)  39.1 us
    unnamed x15, local copies, waits for them, and re-layouts  16.4 us
    all_to_all x1, starting transfers between devices, body(): sky_piece = jnp.concatenate(lax.all_to_all(stack, FREQ, 0, 0), axis=1)  14.9 us
    all_to_all x1, waiting for transfers between devices, sent_to_all(): return lax.all_to_all(copies, axis, split_axis=0, concat_axis=0, tiled=True)  14.5 us
  transfers between devices with their start and end apart: 5, of which 5 were waited for; matrix products, arithmetic and copies ran while one was open for 2% of the time, Pallas kernels for 0%

profile of v1, /device:TPU:8, one launch (start us, length us, event | category | flops | bytes accessed | tf_op | source)
XLA Modules:
  0.0 564.1 jit_solution(16455675858829789407)
XLA Ops:
  6.5 6.4 %stack.8 = bf16[64,1,8,2,4096]{4,3,2,1,0:T(2,128)(2,1)} broadcast(bf16[8,2,4096]{2,1,0:T(2,128)(2,1)} %bitcast.70), dimensions={2,3,4} | broadcast | bytes 8519680 | tf_op jit(solution)/shard_map/stack | solution.py:88
  13.0 0.0 copy-start.6
  13.0 0.0 copy-start
  13.0 14.9 %all-to-all-start = ((bf16[64,1,8,2,4096]{4,3,2,1,0:T(2,128)(2,1)}), bf16[64,1,8,2,4096]{4,3,2,1,0:T(2,128)(2,1)}, u32[]{:S(2)}, u32[]{:S(2)}) async-start(bf16[64,1,8,2,4096]{4,3,2,1,0:T(2,128)(2,1)} %stack.8), calls=%async_computation | async-start | bytes 16777216 | tf_op jit(solution)/shard_map/all_to_all | solution.py:89
  27.9 0.0 copy-done.6
  27.9 0.6 fusion.40
  29.2 0.0 copy-done
  29.2 0.1 fusion.73
  29.3 1.5 slice_bitcast_fusion
  30.8 181.5 %all-to-all-done = bf16[64,1,8,2,4096]{4,3,2,1,0:T(2,128)(2,1)} async-done(((bf16[64,1,8,2,4096]{4,3,2,1,0:T(2,128)(2,1)}), bf16[64,1,8,2,4096]{4,3,2,1,0:T(2,128)(2,1)}, u32[]{:S(2)}, u32[]{:S(2)}) %all-to-all-start) | async-done | bytes 8388640 | tf_op jit(solution)/shard_map/all_to_all | solution.py:89
  212.4 0.0 copy-start.1
  212.4 0.0 copy-start.2
  212.4 16.4 %copy.16 = bf16[64,8,2,4096]{3,1,2,0:T(8,128)(2,1)} copy(bf16[64,8,2,4096]{3,2,1,0:T(2,128)(2,1)} %bitcast.31) | data formatting | bytes 16777216
  228.7 0.0 copy-done.1
  228.7 0.0 copy-done.2
  228.8 0.0 copy-start.3
  228.8 0.0 copy-start.4
  228.8 6.1 %fusion.2 = f32[256,512]{1,0:T(8,128)S(1)} fusion(bf16[512,8192]{1,0:T(8,128)(2,1)} %bitcast.60, f32[]{:T(128)S(6)} %convert_element_type.51, bf16[1,4096,128]{2,1,0:T(8,128)(2,1)S(1)} %copy-done.2, bf16[1,4096,128]{2,1,0:T(8,128)(2,1)S(1)} %fusion.73, bf16[1,4096,128]{2,1,0:T(8,128)(2,1)S(1)} %copy-done.1), kind=kOutput, calls=%fused_computation.7 | convolution fusion | flops 2164391936 | bytes 12058628 | tf_op jit(solution)/shard_map/nc,jcb->jbn/dot_general | solution.py:91
  234.8 1.6 broadcast_in_dim.7
  236.4 4.0 all-to-all-start.1
  240.4 0.0 reduce-scatter.4.cloned.1.call-start
  240.4 0.0 copy-done.3
  240.4 0.0 copy-done.4
  240.5 0.3 fusion.37
  240.8 10.9 %maximum_maximum_fusion = bf16[1,8192,256]{2,1,0:T(8,128)(2,1)} fusion(bf16[1,4096,128]{2,1,0:T(8,128)(2,1)} %get-tuple-element.6, bf16[1,4096,128]{2,1,0:T(8,128)(2,1)S(1)} %fusion.73, bf16[1,4096,128]{2,1,0:T(8,128)(2,1)} %get-tuple-element.5), kind=kLoop, calls=%fused_computation.1 | loop fusion | flops 16777216 | bytes 7340032 | tf_op jit(solution)/shard_map/vmap()/concatenate | solution.py:50
  251.6 0.0 copy-start.5
  251.6 14.5 %all-to-all-done.1 = f32[4,1,256,512]{3,2,1,0:T(8,128)S(1)} async-done(((f32[4,1,256,512]{3,2,1,0:T(8,128)}), f32[4,1,256,512]{3,2,1,0:T(8,128)S(1)}, u32[]{:S(2)}, u32[]{:S(2)}) %all-to-all-start.1) | async-done | bytes 2097184 | tf_op jit(solution)/shard_map/all_to_all | solution.py:13
  266.1 0.2 reduce_sum.19
  266.4 4.9 fusion.27
  271.2 4.9 fusion.31
  276.1 0.0 copy-done.5
  276.1 4.9 fusion.9
  281.0 5.1 fusion.25
  286.0 4.9 fusion.12
  290.9 4.9 fusion.29
  295.8 4.7 fusion.15
  300.5 5.0 fusion.16
  305.6 0.1 copy.11
  305.7 4.6 convolution_bitcast_fusion
  310.3 6.2 %copy.12 = f32[4,4,4,8,2,4096]{5,3,4,2,1,0:T(8,128)} copy(f32[4,4,4,8,2,4096]{5,3,4,1,2,0:T(8,128)S(1)} %convolution_bitcast_fusion) | data formatting | bytes 33554432 | tf_op jit(solution)/shard_map/transpose | solution.py:23
  316.5 0.0 reduce-scatter.4.cloned.1.call-update
  316.5 0.0 reduce-scatter.6.cloned.1.call-start
  316.6 149.7 %reduce-scatter.4.cloned.1.call-done = f32[16,8,2,4096]{3,1,2,0:T(8,128)} async-done(((f32[64,8,2,4096]{3,1,2,0:T(8,128)}), f32[16,8,2,4096]{3,1,2,0:T(8,128)}) %reduce-scatter.4.cloned.1.call-update) | async-done | bytes 4194320 | tf_op jit(solution)/shard_map/reduce_scatter | solution.py:26
  466.2 0.0 reduce-scatter.6.cloned.1.call-update
  466.3 0.0 reduce-scatter.8.cloned.1.call-start
  466.3 52.9 %reduce-scatter.6.cloned.1.call-done = f32[4,8,2,4096]{3,1,2,0:T(8,128)} async-done(((f32[16,8,2,4096]{3,1,2,0:T(8,128)}), f32[4,8,2,4096]{3,1,2,0:T(8,128)}) %reduce-scatter.6.cloned.1.call-update) | async-done | bytes 1048592 | tf_op jit(solution)/shard_map/reduce_scatter | solution.py:26
  519.2 0.0 reduce-scatter.8.cloned.1.call-update
  519.2 36.1 %reduce-scatter.8.cloned.1.call-done = f32[1,8,2,4096]{3,1,2,0:T(8,128)} async-done(((f32[4,8,2,4096]{3,1,2,0:T(8,128)}), f32[1,8,2,4096]{3,1,2,0:T(8,128)}) %reduce-scatter.8.cloned.1.call-update) | async-done | bytes 262160 | tf_op jit(solution)/shard_map/reduce_scatter | solution.py:26
  555.3 1.9 copy.13
  (1 shorter events, 0.0 us)
Async XLA Ops:
  13.0 14.9 %copy-start.6 = (s32[1,4]{1,0:T(1,128)S(1)}, s32[1,4]{1,0:T(1,128)}, u32[]{:S(2)}) copy-start(s32[1,4]{1,0:T(1,128)} %param.9) | copy-start | bytes 52
  13.0 16.2 %copy-start = (bf16[1,1,2,4096,128]{4,3,2,1,0:T(8,128)(2,1)S(1)}, bf16[1,1,2,4096,128]{4,3,2,1,0:T(8,128)(2,1)}, u32[]{:S(2)}) copy-start(bf16[1,1,2,4096,128]{4,3,2,1,0:T(8,128)(2,1)} %param.7) | copy-start | bytes 6291460
  13.0 199.4 %all-to-all-start = ((bf16[64,1,8,2,4096]{4,3,2,1,0:T(2,128)(2,1)}), bf16[64,1,8,2,4096]{4,3,2,1,0:T(2,128)(2,1)}, u32[]{:S(2)}, u32[]{:S(2)}) async-start(bf16[64,1,8,2,4096]{4,3,2,1,0:T(2,128)(2,1)} %stack.8), calls=%async_computation | async-start | bytes 16777216 | tf_op jit(solution)/shard_map/all_to_all | solution.py:89
  212.4 16.4 %copy-start.1 = (bf16[1,4096,128]{2,1,0:T(8,128)(2,1)S(1)}, bf16[1,4096,128]{2,1,0:T(8,128)(2,1)}, u32[]{:S(2)}) copy-start(bf16[1,4096,128]{2,1,0:T(8,128)(2,1)} %get-tuple-element.5) | copy-start | bytes 3145732
  212.4 16.4 %copy-start.2 = (bf16[1,4096,128]{2,1,0:T(8,128)(2,1)S(1)}, bf16[1,4096,128]{2,1,0:T(8,128)(2,1)}, u32[]{:S(2)}) copy-start(bf16[1,4096,128]{2,1,0:T(8,128)(2,1)} %get-tuple-element.6) | copy-start | bytes 3145732
  228.8 11.7 %copy-start.3 = (s32[32,512]{1,0:T(8,128)S(1)}, s32[32,512]{1,0:T(8,128)}, u32[]{:S(2)}) copy-start(s32[32,512]{1,0:T(8,128)} %param.11) | copy-start | bytes 196612
  228.8 11.7 %copy-start.4 = (s32[1,128]{1,0:T(1,128)S(1)}, s32[1,128]{1,0:T(1,128)}, u32[]{:S(2)}) copy-start(s32[1,128]{1,0:T(1,128)} %param.10) | copy-start | bytes 1540
  236.4 29.7 %all-to-all-start.1 = ((f32[4,1,256,512]{3,2,1,0:T(8,128)}), f32[4,1,256,512]{3,2,1,0:T(8,128)S(1)}, u32[]{:S(2)}, u32[]{:S(2)}) async-start(f32[4,1,256,512]{3,2,1,0:T(8,128)} %broadcast_in_dim.7), calls=%async_computation.1 | async-start | bytes 4194304 | tf_op jit(solution)/shard_map/all_to_all | solution.py:13
  240.4 225.8 %reduce-scatter.4.cloned.1.call-start = ((), (), s32[]{:S(2)}) async-start(), calls=%async_computation.5 | async-start | bytes 20971520 | tf_op jit(solution)/shard_map/reduce_scatter | solution.py:26
  251.6 24.5 %copy-start.5 = (bf16[1,2,128,512]{3,2,1,0:T(8,128)(2,1)S(1)}, bf16[1,2,128,512]{3,2,1,0:T(8,128)(2,1)}, u32[]{:S(2)}) copy-start(bf16[1,2,128,512]{3,2,1,0:T(8,128)(2,1)} %param.8) | copy-start | bytes 786436
  316.5 202.7 %reduce-scatter.6.cloned.1.call-start = ((), (), s32[]{:S(2)}) async-start(), calls=%async_computation.6 | async-start | bytes 5242880 | tf_op jit(solution)/shard_map/reduce_scatter | solution.py:26
  466.3 89.0 %reduce-scatter.8.cloned.1.call-start = ((), (), s32[]{:S(2)}) async-start(), calls=%async_computation.7 | async-start | bytes 1310720 | tf_op jit(solution)/shard_map/reduce_scatter | solution.py:26
Sparse Core Ops, SparseCore 0:
  316.6 149.5 reduce-scatter.3
  468.8 50.3 reduce-scatter.5
  521.7 33.5 reduce-scatter.7
